TPU v7x, 32 devices: a whole 2x2x4 slice. The times are simulated.
32 devices in a mesh: aux: 4 (over y, core), orb: 8 (over z, x).
Axes of the slice: x: 2, y: 2, z: 4, core: 2. Of those that a mesh axis runs over, the one named last changes fastest.
Arguments:
- integrals: float32 [2048, 16, 512], P('aux', 'orb'), may hold values from -0.6 to 0.6
- metric: float32 [2048, 2048], P('aux'), may hold values from -1 to 3, as said below
- occ_energy: float32 [16], replicated, may hold values from -1.2 to -0.2
- vir_energy: float32 [512], replicated, may hold values from 0.1 to 2
- pair_orbitals: int32 [128, 2], replicated, may hold values from 0 to 15, as said below
Outputs:
- gradient: float32 [2048, 16, 512], P('aux', 'orb')
Inputs may be any that keep to these rules, and one draw needn't show every extreme that they name: metric is exactly symmetric. `pair_orbitals`: the pairs of one patch use at most one orbital from the block of 2 orbitals of each orb index.
All inputs are finite; a program needn't handle non-finite values.
Results may differ from a plain program's by a relative error of at most 0.0003.
Values sent between devices are 32-bit elements; how exact they have to be, the bound alone decides.
A program may use at most 128 MiB of HBM per device.

v0:
```python
import jax
import jax.numpy as jnp
from jax import lax
from jax.sharding import PartitionSpec as P

highest = lax.Precision.HIGHEST


def body(integrals, metric, occ_energy, vir_energy, pair_orbitals):
    aux_rows, occ_count, vir_count = integrals.shape
    flat_rows = integrals.reshape(aux_rows, occ_count * vir_count)
    fitted = lax.psum_scatter(
        lax.dot_general(
            metric,
            flat_rows,
            (((0,), (0,)), ((), ())),
            precision=highest,
            preferred_element_type=jnp.float32,
        ),
        "aux",
        scatter_dimension=0,
        tiled=True,
    )
    fitted = fitted.reshape(aux_rows, occ_count, vir_count)
    orb_count = lax.axis_size("orb")
    my_index = lax.axis_index("orb")
    pair_count = pair_orbitals.shape[0] // orb_count
    pair_ends = pair_orbitals.reshape(orb_count, 2 * pair_count)
    local_pick = jnp.where(pair_ends // occ_count == my_index, pair_ends % occ_count, -1)
    wanted = jnp.max(local_pick, axis=1)
    chooser = (wanted[:, None] == jnp.arange(occ_count, dtype=jnp.int32)[None, :]).astype(
        jnp.float32
    )
    outgoing = jnp.einsum("to,qoa->qta", chooser, fitted, precision=highest)
    arrived = lax.all_to_all(outgoing, "orb", split_axis=1, concat_axis=1, tiled=True)
    my_pairs = lax.dynamic_slice_in_dim(pair_orbitals, my_index * pair_count, pair_count, 0)
    first_orb = my_pairs[:, 0]
    second_orb = my_pairs[:, 1]
    first_slot = first_orb // occ_count
    second_slot = second_orb // occ_count
    left_block = jnp.take(arrived, first_slot, axis=1)
    right_block = jnp.take(arrived, second_slot, axis=1)
    partial_sums = jnp.einsum("qpa,qpb->pab", left_block, right_block, precision=highest)
    occ_shift = occ_energy[first_orb] + occ_energy[second_orb]
    amp_share = lax.psum_scatter(partial_sums, "aux", scatter_dimension=1, tiled=True)
    share_rows = amp_share.shape[1]
    part_vir = lax.dynamic_slice_in_dim(
        vir_energy, lax.axis_index("aux") * share_rows, share_rows, 0
    )
    denominator = part_vir[None, :, None] + vir_energy[None, None, :] - occ_shift[:, None, None]
    amplitudes = lax.all_gather(-amp_share / denominator, "aux", axis=1, tiled=True)
    to_first = jnp.einsum("qpb,pab->qpa", right_block, amplitudes, precision=highest)
    to_second = jnp.einsum("qpa,pab->qpb", left_block, amplitudes, precision=highest)
    slot_ids = jnp.arange(orb_count, dtype=jnp.int32)
    first_hits = (first_slot[:, None] == slot_ids[None, :]).astype(jnp.float32)
    second_hits = (second_slot[:, None] == slot_ids[None, :]).astype(jnp.float32)
    return_slots = jnp.einsum("qpa,ps->qsa", to_first, first_hits, precision=highest)
    return_slots = return_slots + jnp.einsum(
        "qpa,ps->qsa", to_second, second_hits, precision=highest
    )
    received = lax.all_to_all(return_slots, "orb", split_axis=1, concat_axis=1, tiled=True)
    return jnp.einsum("qta,to->qoa", received, chooser, precision=highest)


def solution(mesh):
    return jax.shard_map(
        body,
        mesh=mesh,
        in_specs=(P("aux", "orb", None), P("aux", None), P(), P(), P()),
        out_specs=P("aux", "orb", None),
        check_vma=False,
    )
```

profile of v0, /device:TPU:0, one launch (start us, length us, event | category | flops | bytes accessed | tf_op | source)
XLA Modules:
  0.0 966.3 jit_solution(3839210725099571797)
XLA Ops:
  6.5 2.1 copy.20
  8.6 17.2 %fusion.48 = f32[2048,1024]{1,0:T(8,128)} fusion(f32[512,2048]{1,0:T(8,128)} %param.8, f32[512,1024]{1,0:T(8,128)S(1)} %bitcast.74), kind=kOutput, calls=%fused_computation.86 | convolution fusion | flops 12884901888 | bytes 14680064 | tf_op jit(solution)/shard_map/dot_general | solution.py:13
  25.9 0.1 reduce_max.14
  26.0 0.1 reduce_max.18
  26.1 74.0 %reduce-scatter.3.cloned.1.call-done = f32[512,1024]{1,0:T(8,128)} async-done(((f32[2048,1024]{1,0:T(8,128)}), f32[512,1024]{1,0:T(8,128)}) %reduce-scatter.3.cloned.1.call-update) | async-done | bytes 2097168 | tf_op jit(solution)/shard_map/reduce_scatter | solution.py:12
  100.1 3.6 reshape.52
  103.7 4.8 convolution_bitcast_fusion
  108.5 8.1 copy.11
  116.6 5.5 all-to-all-start
  122.1 0.0 reduce-scatter.5.cloned.1.call-start
  122.1 0.1 constant_dynamic-slice_fusion
  122.3 182.8 %all-to-all-done = f32[512,8,512]{2,0,1:T(8,128)} async-done(((f32[512,8,512]{2,0,1:T(8,128)}), f32[512,8,512]{2,0,1:T(8,128)}, u32[]{:S(2)}, u32[]{:S(2)}) %all-to-all-start) | async-done | bytes 8388640 | tf_op jit(solution)/shard_map/all_to_all | solution.py:35
  305.1 11.5 %gather_fusion.3 = f32[16,512,512]{2,1,0:T(8,128)} fusion(f32[512,8,512]{2,0,1:T(8,128)} %all-to-all-done, s32[1024]{0:T(1024)S(1)} %get-tuple-element.16), kind=kCustom, calls=%fused_computation.1.clone | custom fusion | bytes 33554496 | tf_op jit(solution)/shard_map/jit(_take)/gather | solution.py:42
  316.6 11.3 %gather_fusion.2 = f32[16,512,512]{2,1,0:T(8,128)} fusion(f32[512,8,512]{2,0,1:T(8,128)} %all-to-all-done, s32[1024]{0:T(1024)S(1)} %get-tuple-element.17), kind=kCustom, calls=%fused_computation.clone | custom fusion | bytes 33554496 | tf_op jit(solution)/shard_map/jit(_take)/gather | solution.py:41
  327.9 35.8 %fusion.2 = f32[16,512,512]{2,1,0:T(8,128)} fusion(f32[16,512,512]{2,1,0:T(8,128)} %gather_fusion.3, f32[16,512,512]{2,1,0:T(8,128)} %gather_fusion.2, pred[16]{0:T(512)(128)(4,1)S(1)} %get-tuple-element.14, pred[16]{0:T(512)(128)(4,1)S(1)} %get-tuple-element.6), kind=kOutput, calls=%fused_computation.6 | convolution fusion | flops 25778192384 | bytes 50331680 | tf_op jit(solution)/shard_map/qpa,qpb->pab/dot_general | solution.py:43
  363.8 0.0 all-gather.2.cloned.1.call-start
  363.9 0.7 gather_fusion.1
  364.5 0.7 gather_fusion
  365.2 0.1 dynamic_slice.7
  365.3 0.1 broadcast_add_fusion
  365.4 121.6 %reduce-scatter.5.cloned.1.call-done = f32[16,128,512]{2,1,0:T(8,128)} async-done(((f32[16,512,512]{2,1,0:T(8,128)}), f32[16,128,512]{2,1,0:T(8,128)}) %reduce-scatter.5.cloned.1.call-update) | async-done | bytes 4194320 | tf_op jit(solution)/shard_map/reduce_scatter | solution.py:45
  487.0 5.0 subtract_divide_fusion
  492.0 106.1 %all-gather.2.cloned.1.call-done = f32[16,512,512]{2,1,0:T(8,128)} async-done(((f32[16,128,512]{2,1,0:T(8,128)}), f32[16,512,512]{2,1,0:T(8,128)}) %all-gather.2.cloned.1.call-update) | async-done | bytes 16777232 | tf_op jit(solution)/shard_map/all_gather | solution.py:51
  598.1 33.9 %fusion.14 = f32[512,16,512]{0,2,1:T(8,128)} fusion(f32[16,512,512]{2,1,0:T(8,128)} %all-gather.2.cloned.1.call-done, f32[16,512,512]{2,1,0:T(8,128)} %gather_fusion.3, pred[16]{0:T(512)(128)(4,1)S(1)} %get-tuple-element.14), kind=kOutput, calls=%fused_computation.16 | convolution fusion | flops 25773998080 | bytes 50331664 | tf_op jit(solution)/shard_map/qpb,pab->qpa/dot_general | solution.py:52
  632.0 20.2 %copy.13 = f32[512,16,512]{2,1,0:T(8,128)} copy(f32[512,16,512]{0,2,1:T(8,128)} %fusion.14) | data formatting | bytes 33554432 | tf_op jit(solution)/shard_map/qpb,pab->qpa/transpose | solution.py:52
  652.2 59.4 %fusion.11 = f32[512,16,512]{0,2,1:T(8,128)} fusion(f32[16,512,512]{2,1,0:T(8,128)} %all-gather.2.cloned.1.call-done, f32[16,512,512]{2,1,0:T(8,128)} %gather_fusion.2, pred[16]{0:T(512)(128)(4,1)S(1)} %get-tuple-element.6), kind=kOutput, calls=%fused_computation.15 | convolution fusion | flops 25773998080 | bytes 50331664 | tf_op jit(solution)/shard_map/qpa,pab->qpb/dot_general | solution.py:53
  711.6 20.3 %copy.15 = f32[512,16,512]{2,1,0:T(8,128)} copy(f32[512,16,512]{0,2,1:T(8,128)} %fusion.11) | data formatting | bytes 33554432 | tf_op jit(solution)/shard_map/qpa,pab->qpb/transpose | solution.py:53
  731.9 9.6 fusion.30
  741.5 12.6 %add_bitcast_fusion = f32[512,8,512]{2,1,0:T(8,128)} fusion(f32[8,512,512]{2,0,1:T(8,128)S(1)} %fusion.30, f32[512,16,512]{2,1,0:T(8,128)} %copy.15, s32[16]{0:T(128)S(1)} %get-tuple-element.10), kind=kOutput, calls=%fused_computation.22 | convolution fusion | flops 404750464 | bytes 33554496 | tf_op jit(solution)/shard_map/qpa,ps->qsa/dot_general | solution.py:58
  754.0 8.2 copy.16
  762.3 188.9 %all_to_all.10 = f32[512,8,512]{2,0,1:T(8,128)S(1)} all-to-all(f32[512,8,512]{2,0,1:T(8,128)S(1)} %copy.16), channel_id=1, replica_groups=mesh['aux'=4,'orb'=8] {'orb'}, dimensions={1} | all-to-all | bytes 16777216 | tf_op jit(solution)/shard_map/all_to_all | solution.py:61
  951.2 8.3 fusion.26
  (18 shorter events, 0.1 us)
Async XLA Ops:
  6.5 357.3 %copy-start = (f32[16]{0:T(128)S(1)}, f32[16]{0:T(128)}, u32[]{:S(2)}) copy-start(f32[16]{0:T(128)} %param.9) | copy-start | bytes 196
  6.5 19.3 %copy-start.2 = (s32[128,2]{0,1:T(2,128)S(1)}, s32[128,2]{0,1:T(2,128)}, u32[]{:S(2)}) copy-start(s32[128,2]{0,1:T(2,128)} %param.11) | copy-start | bytes 3076
  6.5 93.6 %reduce-scatter.3.cloned.1.call-start = ((), (), s32[]{:S(2)}) async-start(), calls=%async_computation.4 | async-start | bytes 10485760 | tf_op jit(solution)/shard_map/reduce_scatter | solution.py:12
  116.6 188.5 %all-to-all-start = ((f32[512,8,512]{2,0,1:T(8,128)}), f32[512,8,512]{2,0,1:T(8,128)}, u32[]{:S(2)}, u32[]{:S(2)}) async-start(f32[512,8,512]{2,0,1:T(8,128)} %copy.11), calls=%async_computation.1 | async-start | bytes 16777216 | tf_op jit(solution)/shard_map/all_to_all | solution.py:35
  122.1 364.9 %reduce-scatter.5.cloned.1.call-start = ((), (), s32[]{:S(2)}) async-start(), calls=%async_computation.5 | async-start | bytes 20971520 | tf_op jit(solution)/shard_map/reduce_scatter | solution.py:45
  363.7 1.5 copy-start.3
  363.8 234.3 %all-gather.2.cloned.1.call-start = ((), (), s32[]{:S(2)}) async-start(), calls=%async_computation.6 | async-start | bytes 20971520 | tf_op jit(solution)/shard_map/all_gather | solution.py:51
  754.0 205.5 %copy-start.1 = (f32[16]{0:T(128)S(1)}, f32[16]{0:T(128)}, u32[]{:S(2)}) copy-start(f32[16]{0:T(128)} %param.9) | copy-start | bytes 196
Sparse Core Ops, SparseCore 0:
  26.0 74.1 reduce-scatter.2
  363.9 123.0 reduce-scatter.4
  492.1 105.8 all-gather.1
where the time goes:
time: 974 us; the launch traced here: 966 us
  waiting for transfers between devices  485 us (50%)
  blocking collectives  189 us (19%)
  matrix products  182 us (19%)
  local copies, waits for them, and re-layouts  86.9 us (9%)
  between operations  13.5 us (1%)
    all_to_all x1, blocking collectives, body(): lax.all_to_all(return_slots, 'orb', split_axis=1, concat_axis=1, tiled=True)  189 us
    all_to_all x1, waiting for transfers between devices, body(): lax.all_to_all(outgoing, 'orb', split_axis=1, concat_axis=1, tiled=True)  183 us
    reduce_scatter x1, waiting for transfers between devices, body(): lax.psum_scatter(partial_sums, 'aux', scatter_dimension=1, tiled=True)  122 us
    all_gather x1, waiting for transfers between devices, body(): lax.all_gather(-amp_share / denominator, 'aux', axis=1, tiled=True)  106 us
    reduce_scatter x1, waiting for transfers between devices, body(): lax.psum_scatter(lax.dot_general(metric, flat_rows, (((0,), (0,)), ((), (...  74 us
    dot_general x1, matrix products, body(): jnp.einsum('qpa,pab->qpb', left_block, amplitudes, precision=highest)  59.4 us
    dot_general x1, matrix products, body(): jnp.einsum('qpa,qpb->pab', left_block, right_block, precision=highest)  35.8 us
    dot_general x1, matrix products, body(): jnp.einsum('qpb,pab->qpa', right_block, amplitudes, precision=highest)  33.9 us
  transfers between devices with their start and end apart: 4, of which 4 were waited for; matrix products, arithmetic and copies ran while one was open for 0% of the time, Pallas kernels for 0%

commit v1 on v0

v1 whole, which is shorter than its diff:
```python
import functools

import jax
import jax.numpy as jnp
from jax import lax
from jax.experimental import pallas as pl
from jax.experimental.pallas import tpu as pltpu
from jax.sharding import PartitionSpec as P

high = lax.Precision.HIGH
MESH = pl.DeviceIdType.MESH
VMEM_LIMIT = 60 * 1024 * 1024
f32 = jnp.float32
bf16 = jnp.bfloat16


def flip(index, step, count):
    total = 0
    bit = 1
    while bit < count:
        total = total + bit * ((index // bit + (step // bit) % 2) % 2)
        bit *= 2
    return total


def spread_order(count):
    far = list(range(count // 2, count))
    near = list(range(1, count // 2))
    far = far[0::2] + far[1::2]
    merged = []
    while far or near:
        if far:
            merged.append(far.pop(0))
        if near:
            merged.append(near.pop(0))
    return merged


def split(value):
    upper = value.astype(bf16)
    lower = (value - upper.astype(f32)).astype(bf16)
    return upper, lower


def dot3(left, right, dims):
    lu, ll = split(left)
    ru, rl = split(right)
    mul = functools.partial(
        lax.dot_general, dimension_numbers=(dims, ((), ())), preferred_element_type=f32
    )
    return mul(lu, ru) + (mul(lu, rl) + mul(ll, ru))


def gather_kernel(
    orb_count,
    y_count,
    exchange,
    x_ref,
    out_ref,
    stage,
    local_sem,
    orb_send,
    orb_recv,
    y_send,
    y_recv,
    c_send,
    c_recv,
):
    aux = lax.axis_index("aux")
    orb = lax.axis_index("orb")
    y = aux // 2
    core = aux % 2
    partner = 2 * y + 1 - core
    blocks = x_ref.shape[0]

    def y_peer(j):
        return 2 * ((y + j) % y_count) + core

    barrier = pltpu.get_barrier_semaphore()
    greeted = 0
    if exchange:
        for k in range(1, orb_count):
            pl.semaphore_signal(
                barrier,
                inc=1,
                device_id={"aux": aux, "orb": flip(orb, k, orb_count)},
                device_id_type=MESH,
            )
            greeted += 1
    for j in range(1, y_count):
        pl.semaphore_signal(
            barrier, inc=1, device_id={"aux": y_peer(j), "orb": orb}, device_id_type=MESH
        )
        greeted += 1
    pl.semaphore_signal(
        barrier, inc=1, device_id={"aux": partner, "orb": orb}, device_id_type=MESH
    )
    greeted += 1
    pl.semaphore_wait(barrier, greeted)

    def orb_copy(k):
        to = flip(orb, k, orb_count)
        return pltpu.make_async_remote_copy(
            src_ref=x_ref.at[to],
            dst_ref=out_ref.at[aux, orb],
            send_sem=orb_send.at[k],
            recv_sem=orb_recv.at[k],
            device_id={"aux": aux, "orb": to},
            device_id_type=MESH,
        )

    def own(k):
        if not exchange:
            return x_ref.at[k], k
        place = flip(orb, k, orb_count)
        if k == 0:
            return x_ref.at[place], place
        return out_ref.at[aux, place], place

    def y_copy(k, j):
        src, place = own(k)
        return pltpu.make_async_remote_copy(
            src_ref=src,
            dst_ref=out_ref.at[aux, place],
            send_sem=y_send.at[j - 1, k],
            recv_sem=y_recv.at[j - 1, k],
            device_id={"aux": y_peer(j), "orb": orb},
            device_id_type=MESH,
        )

    def core_copy(k):
        src, place = own(k)
        return pltpu.make_async_remote_copy(
            src_ref=src,
            dst_ref=out_ref.at[aux, place],
            send_sem=c_send.at[0, k],
            recv_sem=c_recv.at[0, k],
            device_id={"aux": partner, "orb": orb},
            device_id_type=MESH,
        )

    def relay_copy(k, j):
        source = 2 * ((y + y_count - j) % y_count) + core
        place = own(k)[1]
        return pltpu.make_async_remote_copy(
            src_ref=out_ref.at[source, place],
            dst_ref=out_ref.at[source, place],
            send_sem=c_send.at[j, k],
            recv_sem=c_recv.at[j, k],
            device_id={"aux": partner, "orb": orb},
            device_id_type=MESH,
        )

    steps = spread_order(orb_count) if exchange else list(range(1, blocks))
    if exchange:
        for k in steps:
            orb_copy(k).start()
    pending = []

    def relay(k):
        for j in range(1, y_count):
            y_copy(k, j).wait_recv()
            relay_copy(k, j).start()

    for k in [0] + steps:
        if exchange and k:
            orb_copy(k).wait_recv()
        for j in range(1, y_count):
            y_copy(k, j).start()
        core_copy(k).start()
        if k == 0 or not exchange:
            src, place = own(k)
            load = pltpu.make_async_copy(src, stage, local_sem)
            load.start()
            load.wait()
            save = pltpu.make_async_copy(stage, out_ref.at[aux, place], local_sem)
            save.start()
            save.wait()
        pending.append(k)
        if len(pending) > 2:
            relay(pending.pop(0))
    for k in pending:
        relay(k)
    for k in [0] + steps:
        core_copy(k).wait()
        for j in range(1, y_count):
            relay_copy(k, j).wait()
            y_copy(k, j).wait_send()
        if exchange and k:
            orb_copy(k).wait_send()


def gather(blocks, aux_count, exchange, collective_id):
    count = blocks.shape[0]
    y_count = aux_count // 2
    dma = pltpu.SemaphoreType.DMA
    return pl.pallas_call(
        functools.partial(gather_kernel, count, y_count, exchange),
        out_shape=jax.ShapeDtypeStruct((aux_count,) + blocks.shape, f32),
        in_specs=[pl.BlockSpec(memory_space=pl.ANY)],
        out_specs=pl.BlockSpec(memory_space=pl.ANY),
        scratch_shapes=[
            pltpu.VMEM(blocks.shape[1:], f32),
            dma(()),
            dma((count,)),
            dma((count,)),
            dma((y_count - 1, count)),
            dma((y_count - 1, count)),
            dma((y_count, count)),
            dma((y_count, count)),
        ],
        compiler_params=pltpu.CompilerParams(
            collective_id=collective_id, has_side_effects=True, vmem_limit_bytes=VMEM_LIMIT
        ),
        name="gather_exchange" if exchange else "gather_aux",
    )(blocks)


def return_kernel(
    orb_count,
    r_ref,
    out_ref,
    mine,
    theirs,
    sums,
    peer_sums,
    load_sem,
    c_send,
    c_recv,
    y_send,
    y_recv,
    orb_send,
    orb_recv,
    local_sem,
):
    aux = lax.axis_index("aux")
    orb = lax.axis_index("orb")
    y = aux // 2
    core = aux % 2
    partner = 2 * y + 1 - core
    across = 2 * (1 - y) + core
    rows = r_ref.shape[2]
    tile = 64

    barrier = pltpu.get_barrier_semaphore()
    for k in range(1, orb_count):
        pl.semaphore_signal(
            barrier,
            inc=1,
            device_id={"aux": aux, "orb": flip(orb, k, orb_count)},
            device_id_type=MESH,
        )
    for peer in (partner, across):
        pl.semaphore_signal(
            barrier, inc=1, device_id={"aux": peer, "orb": orb}, device_id_type=MESH
        )
    pl.semaphore_wait(barrier, orb_count + 1)

    half = orb_count // 2
    steps = list(range(half, orb_count, 2)) + list(range(half + 1, orb_count, 2))
    steps = steps + list(range(half - 1, 0, -1)) + [0]

    def core_copy(k, side):
        row = y if side == 0 else 1 - y
        return pltpu.make_async_remote_copy(
            src_ref=r_ref.at[2 * row + 1 - core, flip(orb, k, orb_count)],
            dst_ref=theirs.at[side, k],
            send_sem=c_send.at[side, k],
            recv_sem=c_recv.at[side, k],
            device_id={"aux": partner, "orb": orb},
            device_id_type=MESH,
        )

    def load(k, side, slot):
        row = y if side == 0 else 1 - y
        return pltpu.make_async_copy(
            r_ref.at[2 * row + core, flip(orb, k, orb_count)],
            mine.at[slot, side],
            load_sem.at[slot, side],
        )

    def y_copy(k):
        return pltpu.make_async_remote_copy(
            src_ref=sums.at[1, k],
            dst_ref=peer_sums.at[k],
            send_sem=y_send.at[k],
            recv_sem=y_recv.at[k],
            device_id={"aux": across, "orb": orb},
            device_id_type=MESH,
        )

    def orb_copy(k):
        return pltpu.make_async_remote_copy(
            src_ref=sums.at[0, k],
            dst_ref=out_ref.at[orb],
            send_sem=orb_send.at[k],
            recv_sem=orb_recv.at[k],
            device_id={"aux": aux, "orb": flip(orb, k, orb_count)},
            device_id_type=MESH,
        )

    def add(into, left, right):
        def one(i, carry):
            at = pl.ds(pl.multiple_of(i * tile, tile), tile)
            into[at, :] = left[at, :] + right[at, :]
            return carry

        lax.fori_loop(0, rows // tile, one, 0)

    def finish(k):
        y_copy(k).wait_recv()
        add(sums.at[0, k], sums.at[0, k], peer_sums.at[k])
        if k:
            orb_copy(k).start()

    for k in steps:
        for side in (1, 0):
            core_copy(k, side).start()
    for side in (1, 0):
        load(steps[0], side, 0).start()
    pending = []
    for place, k in enumerate(steps):
        slot = place % 2
        if place + 1 < len(steps):
            for side in (1, 0):
                load(steps[place + 1], side, 1 - slot).start()
        for side in (1, 0):
            core_copy(k, side).wait_recv()
            load(k, side, slot).wait()
            add(sums.at[side, k], mine.at[slot, side], theirs.at[side, k])
            if side == 1:
                y_copy(k).start()
        pending.append(k)
        if len(pending) > 2:
            finish(pending.pop(0))
    for k in pending:
        finish(k)
    keep = pltpu.make_async_copy(sums.at[0, 0], out_ref.at[orb], local_sem)
    keep.start()
    keep.wait()
    for k in steps:
        for side in (1, 0):
            core_copy(k, side).wait_send()
        y_copy(k).wait_send()
        if k:
            orb_copy(k).wait()


def give_back(contributions, collective_id):
    _, orb_count, rows, cols = contributions.shape
    dma = pltpu.SemaphoreType.DMA
    return pl.pallas_call(
        functools.partial(return_kernel, orb_count),
        out_shape=jax.ShapeDtypeStruct((orb_count, rows, cols), f32),
        in_specs=[pl.BlockSpec(memory_space=pl.ANY)],
        out_specs=pl.BlockSpec(memory_space=pl.ANY),
        scratch_shapes=[
            pltpu.VMEM((2, 2, rows, cols), f32),
            pltpu.VMEM((2, orb_count, rows, cols), f32),
            pltpu.VMEM((2, orb_count, rows, cols), f32),
            pltpu.VMEM((orb_count, rows, cols), f32),
            dma((2, 2)),
            dma((2, orb_count)),
            dma((2, orb_count)),
            dma((orb_count,)),
            dma((orb_count,)),
            dma((orb_count,)),
            dma((orb_count,)),
            dma(()),
        ],
        compiler_params=pltpu.CompilerParams(
            collective_id=collective_id, has_side_effects=True, vmem_limit_bytes=VMEM_LIMIT
        ),
        name="give_back",
    )(contributions)


def amplitude_kernel(first_ref, second_ref, shift_ref, left, right, col, row, out, total):
    pair = pl.program_id(0)
    step = pl.program_id(1)

    @pl.when(step == 0)
    def _():
        total[...] = jnp.zeros_like(total)

    total[...] += dot3(left[0, 0], right[0, 0], ((0,), (0,)))

    @pl.when(step == pl.num_programs(1) - 1)
    def _():
        out[0] = -total[...] / (col[...] + row[...] - shift_ref[pair])


def amplitudes_of(first_slot, second_slot, shift, slots, vir_energy):
    pairs = first_slot.shape[0]
    aux_count, _, rows, cols = slots.shape
    return pl.pallas_call(
        amplitude_kernel,
        grid_spec=pltpu.PrefetchScalarGridSpec(
            num_scalar_prefetch=3,
            grid=(pairs, aux_count),
            in_specs=[
                pl.BlockSpec((1, 1, rows, cols), lambda p, a, f, s, e: (a, f[p], 0, 0)),
                pl.BlockSpec((1, 1, rows, cols), lambda p, a, f, s, e: (a, s[p], 0, 0)),
                pl.BlockSpec((cols, 1), lambda p, a, f, s, e: (0, 0)),
                pl.BlockSpec((1, cols), lambda p, a, f, s, e: (0, 0)),
            ],
            out_specs=pl.BlockSpec((1, cols, cols), lambda p, a, f, s, e: (p, 0, 0)),
            scratch_shapes=[pltpu.VMEM((cols, cols), f32)],
        ),
        out_shape=jax.ShapeDtypeStruct((pairs, cols, cols), f32),
        compiler_params=pltpu.CompilerParams(vmem_limit_bytes=VMEM_LIMIT),
        name="pair_amplitudes",
    )(first_slot, second_slot, shift, slots, slots, vir_energy[:, None], vir_energy[None, :])


def contribution_kernel(first_ref, second_ref, slots, amps, out):
    slot = pl.program_id(1)
    out[0, 0] = jnp.zeros_like(out[0, 0])

    def visit(pair, carry):
        first = first_ref[pair]
        second = second_ref[pair]

        @pl.when(first == slot)
        def _():
            out[0, 0] += dot3(slots[0, second], amps[pair], ((1,), (1,)))

        @pl.when(second == slot)
        def _():
            out[0, 0] += dot3(slots[0, first], amps[pair], ((1,), (0,)))

        return carry

    lax.fori_loop(0, amps.shape[0], visit, 0)


def contributions_of(first_slot, second_slot, slots, amps):
    aux_count, orb_count, rows, cols = slots.shape
    return pl.pallas_call(
        contribution_kernel,
        grid_spec=pltpu.PrefetchScalarGridSpec(
            num_scalar_prefetch=2,
            grid=(aux_count, orb_count),
            in_specs=[
                pl.BlockSpec((1, orb_count, rows, cols), lambda a, o, f, s: (a, 0, 0, 0)),
                pl.BlockSpec(amps.shape, lambda a, o, f, s: (0, 0, 0)),
            ],
            out_specs=pl.BlockSpec((1, 1, rows, cols), lambda a, o, f, s: (a, o, 0, 0)),
        ),
        out_shape=jax.ShapeDtypeStruct(slots.shape, f32),
        compiler_params=pltpu.CompilerParams(vmem_limit_bytes=VMEM_LIMIT),
        name="slot_contributions",
    )(first_slot, second_slot, slots, amps)


def body(integrals, metric, occ_energy, vir_energy, pair_orbitals):
    aux_rows, occ_count, vir_count = integrals.shape
    aux_count = lax.axis_size("aux")
    orb_count = lax.axis_size("orb")
    aux_index = lax.axis_index("aux")
    orb_index = lax.axis_index("orb")
    pieces = 4
    columns = occ_count * vir_count
    all_rows = gather(
        integrals.reshape(pieces, aux_rows // pieces, columns), aux_count, False, 1
    ).reshape(aux_count * aux_rows, columns)
    fitted = lax.dot_general(
        metric, all_rows, (((1,), (0,)), ((), ())), precision=high, preferred_element_type=f32
    )
    pair_count = pair_orbitals.shape[0] // orb_count
    pair_ends = pair_orbitals.reshape(orb_count, 2 * pair_count)
    local_pick = jnp.where(pair_ends // occ_count == orb_index, pair_ends % occ_count, -1)
    wanted = jnp.max(local_pick, axis=1)
    outgoing = jnp.zeros((orb_count, aux_rows, vir_count), f32)
    for o in range(occ_count):
        part = fitted[:, o * vir_count : (o + 1) * vir_count]
        outgoing = jnp.where((wanted == o)[:, None, None], part[None], outgoing)
    slots = gather(outgoing, aux_count, True, 2)
    my_count = pair_count // aux_count
    my_pairs = lax.dynamic_slice_in_dim(
        pair_orbitals, orb_index * pair_count + aux_index * my_count, my_count, 0
    )
    first_orb = my_pairs[:, 0]
    second_orb = my_pairs[:, 1]
    first_slot = first_orb // occ_count
    second_slot = second_orb // occ_count
    shift = occ_energy[first_orb] + occ_energy[second_orb]
    amps = amplitudes_of(first_slot, second_slot, shift, slots, vir_energy)
    contributions = contributions_of(first_slot, second_slot, slots, amps)
    received = give_back(contributions, 3)
    outs = [
        jnp.sum(jnp.where((wanted == o)[:, None, None], received, 0.0), axis=0)
        for o in range(occ_count)
    ]
    return jnp.stack(outs, axis=1)


def plain_body(integrals, metric, occ_energy, vir_energy, pair_orbitals):
    aux_rows, occ_count, vir_count = integrals.shape
    flat_rows = integrals.reshape(aux_rows, occ_count * vir_count)
    fitted = lax.psum_scatter(
        lax.dot_general(
            metric, flat_rows, (((0,), (0,)), ((), ())), precision=high, preferred_element_type=f32
        ),
        "aux",
        scatter_dimension=0,
        tiled=True,
    )
    fitted = fitted.reshape(aux_rows, occ_count, vir_count)
    orb_count = lax.axis_size("orb")
    my_index = lax.axis_index("orb")
    pair_count = pair_orbitals.shape[0] // orb_count
    pair_ends = pair_orbitals.reshape(orb_count, 2 * pair_count)
    local_pick = jnp.where(pair_ends // occ_count == my_index, pair_ends % occ_count, -1)
    wanted = jnp.max(local_pick, axis=1)
    chooser = (wanted[:, None] == jnp.arange(occ_count, dtype=jnp.int32)[None, :]).astype(f32)
    outgoing = jnp.einsum("to,qoa->qta", chooser, fitted, precision=high)
    arrived = lax.all_to_all(outgoing, "orb", split_axis=1, concat_axis=1, tiled=True)
    my_pairs = lax.dynamic_slice_in_dim(pair_orbitals, my_index * pair_count, pair_count, 0)
    first_orb = my_pairs[:, 0]
    second_orb = my_pairs[:, 1]
    first_slot = first_orb // occ_count
    second_slot = second_orb // occ_count
    left_block = jnp.take(arrived, first_slot, axis=1)
    right_block = jnp.take(arrived, second_slot, axis=1)
    partial_sums = jnp.einsum("qpa,qpb->pab", left_block, right_block, precision=high)
    occ_shift = occ_energy[first_orb] + occ_energy[second_orb]
    amp_share = lax.psum_scatter(partial_sums, "aux", scatter_dimension=1, tiled=True)
    share_rows = amp_share.shape[1]
    part_vir = lax.dynamic_slice_in_dim(
        vir_energy, lax.axis_index("aux") * share_rows, share_rows, 0
    )
    denominator = part_vir[None, :, None] + vir_energy[None, None, :] - occ_shift[:, None, None]
    amplitudes = lax.all_gather(-amp_share / denominator, "aux", axis=1, tiled=True)
    to_first = jnp.einsum("qpb,pab->qpa", right_block, amplitudes, precision=high)
    to_second = jnp.einsum("qpa,pab->qpb", left_block, amplitudes, precision=high)
    slot_ids = jnp.arange(orb_count, dtype=jnp.int32)
    first_hits = (first_slot[:, None] == slot_ids[None, :]).astype(f32)
    second_hits = (second_slot[:, None] == slot_ids[None, :]).astype(f32)
    return_slots = jnp.einsum("qpa,ps->qsa", to_first, first_hits, precision=high)
    return_slots = return_slots + jnp.einsum(
        "qpa,ps->qsa", to_second, second_hits, precision=high
    )
    received = lax.all_to_all(return_slots, "orb", split_axis=1, concat_axis=1, tiled=True)
    return jnp.einsum("qta,to->qoa", received, chooser, precision=high)


def solution(mesh):
    aux_count = mesh.shape["aux"]
    orb_count = mesh.shape["orb"]

    def step(integrals, metric, occ_energy, vir_energy, pair_orbitals):
        slot_bytes = 4 * metric.shape[1] * integrals.shape[2] * orb_count
        fits = 2 * slot_bytes <= 64 * 1024 * 1024
        power = orb_count & (orb_count - 1) == 0
        whole_pairs = pair_orbitals.shape[0] % (orb_count * aux_count) == 0
        chosen = body if fits and power and whole_pairs and aux_count == 4 else plain_body
        return jax.shard_map(
            chosen,
            mesh=mesh,
            in_specs=(P("aux", "orb", None), P("aux", None), P(), P(), P()),
            out_specs=P("aux", "orb", None),
            check_vma=False,
        )(integrals, metric, occ_energy, vir_energy, pair_orbitals)

    return step
```

time: 974 us -> 624 us (0.64)
  Pallas kernels: 0 us -> 588 us
  waiting for transfers between devices: 485 us -> 0 us
  blocking collectives: 189 us -> 0 us
  matrix products: 182 us -> 10.8 us
  local copies, waits for them, and re-layouts: 86.9 us -> 10.8 us
  between operations: 13.5 us -> 0.09 us
    pallas_call x0 -> x5, Pallas kernels: none -> 588 us  [the longest x2 289 us: gather(): pl.pallas_call(functools.partial(gather_kernel, count, y_count, exchange)...]
    reduce_scatter x2 -> x0, waiting for transfers between devices: 196 us -> none  [the longest x1 122 us: body(): lax.psum_scatter(partial_sums, 'aux', scatter_dimension=1, tiled=True)]
    all_to_all x1 -> x0, blocking collectives: 189 us -> none  [body(): lax.all_to_all(return_slots, 'orb', split_axis=1, concat_axis=1, tiled=True)]
    all_to_all x1 -> x0, waiting for transfers between devices: 183 us -> none  [body(): lax.all_to_all(outgoing, 'orb', split_axis=1, concat_axis=1, tiled=True)]
    dot_general x8 -> x1, matrix products: 182 us -> 10.8 us  [body(): lax.dot_general(metric, all_rows, (((1,), (0,)), ((), ())), precision=hig...]
    all_gather x1 -> x0, waiting for transfers between devices: 106 us -> none  [body(): lax.all_gather(-amp_share / denominator, 'aux', axis=1, tiled=True)]
    transpose x3 -> x0, local copies, waits for them, and re-layouts: 48.6 us -> none  [the longest x1 20.3 us: body(): jnp.einsum('qpa,pab->qpb', left_block, amplitudes, precision=highest)]
    gather x4 -> x2, local copies, waits for them, and re-layouts: 24.1 us -> 1.28 us  [body(): shift = occ_energy[first_orb] + occ_energy[second_orb]]
  transfers between devices with their start and end apart: 4 -> 0, of which waited for: 4 -> 0; matrix products, arithmetic and copies ran while one was open for 0% -> 0% of each run, Pallas kernels for 0% -> 0%
where the time goes in v1:
time: 624 us; the launch traced here: 622 us
  Pallas kernels  588 us (94%)
  other arithmetic  11.5 us (2%)
  local copies, waits for them, and re-layouts  10.8 us (2%)
  matrix products  10.8 us (2%)
    pallas_call x2, Pallas kernels, gather(): pl.pallas_call(functools.partial(gather_kernel, count, y_count, exchange)...  289 us
    pallas_call x1, Pallas kernels, give_back(): pl.pallas_call(functools.partial(return_kernel, orb_count), out_shape=jax...  214 us
    pallas_call x1, Pallas kernels, contributions_of(): pl.pallas_call(contribution_kernel, grid_spec=pltpu.PrefetchScalarGridSpe...  59.3 us
    pallas_call x1, Pallas kernels, amplitudes_of(): pl.pallas_call(amplitude_kernel, grid_spec=pltpu.PrefetchScalarGridSpec(n...  25.8 us

profile of v1, /device:TPU:0, one launch (start us, length us, event | category | flops | bytes accessed | tf_op | source)
XLA Modules:
  0.0 621.5 jit_solution(14387453822468924912)
XLA Ops:
  0.0 0.0 copy-start
  0.0 0.7 fusion
  0.7 0.8 constant_dynamic-slice_fusion
  1.5 0.6 and_select_fusion
  2.1 0.1 reduce_max.14
  2.1 0.1 reduce_max.18
  2.3 0.0 copy-done
  2.3 0.6 gather_fusion.1
  2.9 0.6 gather_fusion
  3.6 0.5 add.33.shift_ref
  4.1 1.5 copy.6.col
  5.7 4.0 reshape.16.x_ref
  9.7 51.8 %gather_aux.1 = f32[4,4,128,1024]{3,2,1,0:T(8,128)} custom-call(f32[4,128,1024]{2,1,0:T(8,128)} %reshape.16.x_ref), custom_call_target="tpu_custom_call" | custom-call | tf_op jit(solution)/shard_map/gather_aux/pallas_call | solution.py:197
  61.5 10.8 %fusion.4 = f32[512,1024]{1,0:T(8,128)S(1)} fusion(f32[512,2048]{1,0:T(8,128)} %param.6, f32[2048,1024]{1,0:T(8,128)} %bitcast.27), kind=kOutput, calls=%fused_computation.33 | convolution fusion | flops 6442450944 | bytes 14680064 | tf_op jit(solution)/shard_map/dot_general | solution.py:467
  72.3 0.2 fusion.3
  72.5 4.3 select_select_fusion.x_ref
  76.9 237.1 %gather_exchange.1.left.right.slots = f32[4,8,512,512]{3,2,1,0:T(8,128)} custom-call(f32[8,512,512]{2,1,0:T(8,128)} %select_select_fusion.x_ref), custom_call_target="tpu_custom_call" | custom-call | tf_op jit(solution)/shard_map/gather_exchange/pallas_call | solution.py:197
  314.0 25.8 %pair_amplitudes.1.amps = f32[4,512,512]{2,1,0:T(8,128)} custom-call(s32[4]{0:T(128)} %get-tuple-element.12.first_ref, s32[4]{0:T(128)} %get-tuple-element.11.second_ref, f32[4]{0:T(128)} %add.33.shift_ref, f32[4,8,512,512]{3,2,1,0:T(8,128)} %gather_exchange.1.left.right.slots, f32[4,8,512,512]{3,2,1,0:T(8,128)} %gather_exchange.1.left.right.slots, ...), custom_call_target="tpu_custom_call" | custom-call | tf_op jit(solution)/shard_map/pair_amplitudes/pallas_call | solution.py:396
  339.8 59.3 %slot_contributions.1.r_ref = f32[4,8,512,512]{3,2,1,0:T(8,128)} custom-call(s32[4]{0:T(128)} %get-tuple-element.12.first_ref, s32[4]{0:T(128)} %get-tuple-element.11.second_ref, f32[4,8,512,512]{3,2,1,0:T(8,128)} %gather_exchange.1.left.right.slots, f32[4,512,512]{2,1,0:T(8,128)} %pair_amplitudes.1.amps), custom_call_target="tpu_custom_call" | custom-call | tf_op jit(solution)/shard_map/slot_contributions/pallas_call | solution.py:439
  399.1 214.3 %give_back.1 = f32[8,512,512]{2,1,0:T(8,128)} custom-call(f32[4,8,512,512]{3,2,1,0:T(8,128)} %slot_contributions.1.r_ref), custom_call_target="tpu_custom_call" | custom-call | tf_op jit(solution)/shard_map/give_back/pallas_call | solution.py:352
  613.4 5.0 select_reduce_fusion.1
  618.4 0.0 copy-start.1
  618.4 0.2 pad_maximum_fusion
  618.6 2.9 copy.7
  621.5 0.0 copy-done.1
  (3 shorter events, 0.0 us)
Async XLA Ops:
  0.0 2.3 copy-start
  618.4 3.1 copy-start.1

commit v2 on v1

--- a/solution.py
+++ b/solution.py
@@ -25,9 +25,9 @@
 
 def spread_order(count):
     far = list(range(count // 2, count))
-    near = list(range(1, count // 2))
+    near = list(range(2, count // 2))
     far = far[0::2] + far[1::2]
-    merged = []
+    merged = [1]
     while far or near:
         if far:
             merged.append(far.pop(0))
@@ -43,12 +43,14 @@
 
 
 def dot3(left, right, dims):
-    lu, ll = split(left)
-    ru, rl = split(right)
-    mul = functools.partial(
-        lax.dot_general, dimension_numbers=(dims, ((), ())), preferred_element_type=f32
-    )
-    return mul(lu, ru) + (mul(lu, rl) + mul(ll, ru))
+    (lu, ll), (ru, rl) = left, right
+    (la,), (ra,) = dims
+    return lax.dot_general(
+        jnp.concatenate([lu, lu, ll], axis=la),
+        jnp.concatenate([ru, rl, ru], axis=ra),
+        (dims, ((), ())),
+        preferred_element_type=f32,
+    )
 
 
 def gather_kernel(
@@ -58,7 +60,7 @@
     x_ref,
     out_ref,
     stage,
-    local_sem,
+    keep_sem,
     orb_send,
     orb_recv,
     y_send,
@@ -98,101 +100,114 @@
     greeted += 1
     pl.semaphore_wait(barrier, greeted)
 
-    def orb_copy(k):
+    def orb_copy(k, h):
         to = flip(orb, k, orb_count)
         return pltpu.make_async_remote_copy(
-            src_ref=x_ref.at[to],
-            dst_ref=out_ref.at[aux, orb],
-            send_sem=orb_send.at[k],
-            recv_sem=orb_recv.at[k],
+            src_ref=x_ref.at[to, h],
+            dst_ref=out_ref.at[aux, orb, h],
+            send_sem=orb_send.at[k, h],
+            recv_sem=orb_recv.at[k, h],
             device_id={"aux": aux, "orb": to},
             device_id_type=MESH,
         )
 
-    def own(k):
-        if not exchange:
-            return x_ref.at[k], k
-        place = flip(orb, k, orb_count)
-        if k == 0:
-            return x_ref.at[place], place
-        return out_ref.at[aux, place], place
-
-    def y_copy(k, j):
-        src, place = own(k)
-        return pltpu.make_async_remote_copy(
-            src_ref=src,
-            dst_ref=out_ref.at[aux, place],
-            send_sem=y_send.at[j - 1, k],
-            recv_sem=y_recv.at[j - 1, k],
+    def place_of(k):
+        return flip(orb, k, orb_count) if exchange else k
+
+    def own(k, h):
+        if not exchange or k == 0:
+            return x_ref.at[place_of(k), h]
+        return out_ref.at[aux, place_of(k), h]
+
+    def y_copy(k, h, j):
+        return pltpu.make_async_remote_copy(
+            src_ref=own(k, h),
+            dst_ref=out_ref.at[aux, place_of(k), h],
+            send_sem=y_send.at[j - 1, k, h],
+            recv_sem=y_recv.at[j - 1, k, h],
             device_id={"aux": y_peer(j), "orb": orb},
             device_id_type=MESH,
         )
 
-    def core_copy(k):
-        src, place = own(k)
-        return pltpu.make_async_remote_copy(
-            src_ref=src,
-            dst_ref=out_ref.at[aux, place],
-            send_sem=c_send.at[0, k],
-            recv_sem=c_recv.at[0, k],
+    def core_copy(k, h):
+        return pltpu.make_async_remote_copy(
+            src_ref=own(k, h),
+            dst_ref=out_ref.at[aux, place_of(k), h],
+            send_sem=c_send.at[0, k, h],
+            recv_sem=c_recv.at[0, k, h],
             device_id={"aux": partner, "orb": orb},
             device_id_type=MESH,
         )
 
-    def relay_copy(k, j):
+    def relay_copy(k, h, j):
         source = 2 * ((y + y_count - j) % y_count) + core
-        place = own(k)[1]
-        return pltpu.make_async_remote_copy(
-            src_ref=out_ref.at[source, place],
-            dst_ref=out_ref.at[source, place],
-            send_sem=c_send.at[j, k],
-            recv_sem=c_recv.at[j, k],
+        return pltpu.make_async_remote_copy(
+            src_ref=out_ref.at[source, place_of(k), h],
+            dst_ref=out_ref.at[source, place_of(k), h],
+            send_sem=c_send.at[j, k, h],
+            recv_sem=c_recv.at[j, k, h],
             device_id={"aux": partner, "orb": orb},
             device_id_type=MESH,
         )
 
     steps = spread_order(orb_count) if exchange else list(range(1, blocks))
+    units = [(k, h) for k in [0] + steps for h in range(x_ref.shape[1])]
     if exchange:
-        for k in steps:
-            orb_copy(k).start()
+        for k, h in units:
+            if k:
+                orb_copy(k, h).start()
     pending = []
 
-    def relay(k):
+    def relay(k, h):
         for j in range(1, y_count):
-            y_copy(k, j).wait_recv()
-            relay_copy(k, j).start()
-
-    for k in [0] + steps:
+            y_copy(k, h, j).wait_recv()
+            relay_copy(k, h, j).start()
+
+    def keep_loads():
+        return [
+            pltpu.make_async_copy(own(k, h), stage.at[i], keep_sem.at[i])
+            for i, (k, h) in enumerate(keeps)
+        ]
+
+    def keep_saves():
+        return [
+            pltpu.make_async_copy(stage.at[i], out_ref.at[aux, place_of(k), h], keep_sem.at[i])
+            for i, (k, h) in enumerate(keeps)
+        ]
+
+    keeps = [(k, h) for k, h in units if k == 0 or not exchange]
+    for copy in keep_loads():
+        copy.start()
+    for index, (k, h) in enumerate(units):
         if exchange and k:
-            orb_copy(k).wait_recv()
+            orb_copy(k, h).wait_recv()
         for j in range(1, y_count):
-            y_copy(k, j).start()
-        core_copy(k).start()
-        if k == 0 or not exchange:
-            src, place = own(k)
-            load = pltpu.make_async_copy(src, stage, local_sem)
-            load.start()
-            load.wait()
-            save = pltpu.make_async_copy(stage, out_ref.at[aux, place], local_sem)
-            save.start()
-            save.wait()
-        pending.append(k)
+            y_copy(k, h, j).start()
+        core_copy(k, h).start()
+        pending.append((k, h))
         if len(pending) > 2:
-            relay(pending.pop(0))
-    for k in pending:
-        relay(k)
-    for k in [0] + steps:
-        core_copy(k).wait()
+            relay(*pending.pop(0))
+        if index == len(keeps) - 1:
+            for load, save in zip(keep_loads(), keep_saves()):
+                load.wait()
+                save.start()
+    for unit in pending:
+        relay(*unit)
+    for k, h in units:
+        core_copy(k, h).wait()
         for j in range(1, y_count):
-            relay_copy(k, j).wait()
-            y_copy(k, j).wait_send()
+            relay_copy(k, h, j).wait()
+            y_copy(k, h, j).wait_send()
         if exchange and k:
-            orb_copy(k).wait_send()
+            orb_copy(k, h).wait_send()
+    for save in keep_saves():
+        save.wait()
 
 
 def gather(blocks, aux_count, exchange, collective_id):
-    count = blocks.shape[0]
+    count, parts = blocks.shape[:2]
     y_count = aux_count // 2
+    kept = parts if exchange else count * parts
     dma = pltpu.SemaphoreType.DMA
     return pl.pallas_call(
         functools.partial(gather_kernel, count, y_count, exchange),
@@ -200,14 +215,14 @@
         in_specs=[pl.BlockSpec(memory_space=pl.ANY)],
         out_specs=pl.BlockSpec(memory_space=pl.ANY),
         scratch_shapes=[
-            pltpu.VMEM(blocks.shape[1:], f32),
-            dma(()),
-            dma((count,)),
-            dma((count,)),
-            dma((y_count - 1, count)),
-            dma((y_count - 1, count)),
-            dma((y_count, count)),
-            dma((y_count, count)),
+            pltpu.VMEM((kept,) + blocks.shape[2:], f32),
+            dma((kept,)),
+            dma((count, parts)),
+            dma((count, parts)),
+            dma((y_count - 1, count, parts)),
+            dma((y_count - 1, count, parts)),
+            dma((y_count, count, parts)),
+            dma((y_count, count, parts)),
         ],
         compiler_params=pltpu.CompilerParams(
             collective_id=collective_id, has_side_effects=True, vmem_limit_bytes=VMEM_LIMIT
@@ -231,7 +246,7 @@
     y_recv,
     orb_send,
     orb_recv,
-    local_sem,
+    keep_sem,
 ):
     aux = lax.axis_index("aux")
     orb = lax.axis_index("orb")
@@ -239,7 +254,7 @@
     core = aux % 2
     partner = 2 * y + 1 - core
     across = 2 * (1 - y) + core
-    rows = r_ref.shape[2]
+    parts, rows = r_ref.shape[2:4]
     tile = 64
 
     barrier = pltpu.get_barrier_semaphore()
@@ -256,48 +271,49 @@
         )
     pl.semaphore_wait(barrier, orb_count + 1)
 
-    half = orb_count // 2
-    steps = list(range(half, orb_count, 2)) + list(range(half + 1, orb_count, 2))
-    steps = steps + list(range(half - 1, 0, -1)) + [0]
-
-    def core_copy(k, side):
+    steps = [(k, h) for k in spread_order(orb_count)[1:] + [1, 0] for h in range(parts)]
+
+    def core_copy(k, h, side):
         row = y if side == 0 else 1 - y
         return pltpu.make_async_remote_copy(
-            src_ref=r_ref.at[2 * row + 1 - core, flip(orb, k, orb_count)],
-            dst_ref=theirs.at[side, k],
-            send_sem=c_send.at[side, k],
-            recv_sem=c_recv.at[side, k],
+            src_ref=r_ref.at[2 * row + 1 - core, flip(orb, k, orb_count), h],
+            dst_ref=theirs.at[side, k, h],
+            send_sem=c_send.at[side, k, h],
+            recv_sem=c_recv.at[side, k, h],
             device_id={"aux": partner, "orb": orb},
             device_id_type=MESH,
         )
 
-    def load(k, side, slot):
+    def load(k, h, side, slot):
         row = y if side == 0 else 1 - y
         return pltpu.make_async_copy(
-            r_ref.at[2 * row + core, flip(orb, k, orb_count)],
+            r_ref.at[2 * row + core, flip(orb, k, orb_count), h],
             mine.at[slot, side],
             load_sem.at[slot, side],
         )
 
-    def y_copy(k):
-        return pltpu.make_async_remote_copy(
-            src_ref=sums.at[1, k],
-            dst_ref=peer_sums.at[k],
-            send_sem=y_send.at[k],
-            recv_sem=y_recv.at[k],
+    def y_copy(k, h):
+        return pltpu.make_async_remote_copy(
+            src_ref=sums.at[1, k, h],
+            dst_ref=peer_sums.at[k, h],
+            send_sem=y_send.at[k, h],
+            recv_sem=y_recv.at[k, h],
             device_id={"aux": across, "orb": orb},
             device_id_type=MESH,
         )
 
-    def orb_copy(k):
-        return pltpu.make_async_remote_copy(
-            src_ref=sums.at[0, k],
-            dst_ref=out_ref.at[orb],
-            send_sem=orb_send.at[k],
-            recv_sem=orb_recv.at[k],
+    def orb_copy(k, h):
+        return pltpu.make_async_remote_copy(
+            src_ref=sums.at[0, k, h],
+            dst_ref=out_ref.at[orb, h],
+            send_sem=orb_send.at[k, h],
+            recv_sem=orb_recv.at[k, h],
             device_id={"aux": aux, "orb": flip(orb, k, orb_count)},
             device_id_type=MESH,
         )
+
+    def keep(h):
+        return pltpu.make_async_copy(sums.at[0, 0, h], out_ref.at[orb, h], keep_sem.at[h])
 
     def add(into, left, right):
         def one(i, carry):
@@ -307,66 +323,68 @@
 
         lax.fori_loop(0, rows // tile, one, 0)
 
-    def finish(k):
-        y_copy(k).wait_recv()
-        add(sums.at[0, k], sums.at[0, k], peer_sums.at[k])
+    def finish(k, h):
+        y_copy(k, h).wait_recv()
+        add(sums.at[0, k, h], sums.at[0, k, h], peer_sums.at[k, h])
         if k:
-            orb_copy(k).start()
-
-    for k in steps:
+            orb_copy(k, h).start()
+        else:
+            keep(h).start()
+
+    for k, h in steps:
         for side in (1, 0):
-            core_copy(k, side).start()
+            core_copy(k, h, side).start()
     for side in (1, 0):
-        load(steps[0], side, 0).start()
+        load(*steps[0], side, 0).start()
     pending = []
-    for place, k in enumerate(steps):
+    for place, (k, h) in enumerate(steps):
         slot = place % 2
         if place + 1 < len(steps):
             for side in (1, 0):
-                load(steps[place + 1], side, 1 - slot).start()
+                load(*steps[place + 1], side, 1 - slot).start()
         for side in (1, 0):
-            core_copy(k, side).wait_recv()
-            load(k, side, slot).wait()
-            add(sums.at[side, k], mine.at[slot, side], theirs.at[side, k])
+            core_copy(k, h, side).wait_recv()
+            load(k, h, side, slot).wait()
+            add(sums.at[side, k, h], mine.at[slot, side], theirs.at[side, k, h])
             if side == 1:
-                y_copy(k).start()
-        pending.append(k)
+                y_copy(k, h).start()
+        pending.append((k, h))
         if len(pending) > 2:
-            finish(pending.pop(0))
-    for k in pending:
-        finish(k)
-    keep = pltpu.make_async_copy(sums.at[0, 0], out_ref.at[orb], local_sem)
-    keep.start()
-    keep.wait()
-    for k in steps:
+            finish(*pending.pop(0))
+    for unit in pending:
+        finish(*unit)
+    for k, h in steps:
         for side in (1, 0):
-            core_copy(k, side).wait_send()
-        y_copy(k).wait_send()
+            core_copy(k, h, side).wait_send()
+        y_copy(k, h).wait_send()
         if k:
-            orb_copy(k).wait()
+            orb_copy(k, h).wait()
+        else:
+            keep(h).wait()
 
 
 def give_back(contributions, collective_id):
-    _, orb_count, rows, cols = contributions.shape
+    orb_count, parts, rows, cols = contributions.shape[1:]
+    whole = (orb_count, parts, rows, cols)
     dma = pltpu.SemaphoreType.DMA
     return pl.pallas_call(
         functools.partial(return_kernel, orb_count),
-        out_shape=jax.ShapeDtypeStruct((orb_count, rows, cols), f32),
+        out_shape=jax.ShapeDtypeStruct(whole, f32),
         in_specs=[pl.BlockSpec(memory_space=pl.ANY)],
         out_specs=pl.BlockSpec(memory_space=pl.ANY),
         scratch_shapes=[
             pltpu.VMEM((2, 2, rows, cols), f32),
-            pltpu.VMEM((2, orb_count, rows, cols), f32),
-            pltpu.VMEM((2, orb_count, rows, cols), f32),
-            pltpu.VMEM((orb_count, rows, cols), f32),
+            pltpu.VMEM((2,) + whole, f32),
+            pltpu.VMEM((2,) + whole, f32),
+            pltpu.VMEM(whole, f32),
             dma((2, 2)),
-            dma((2, orb_count)),
-            dma((2, orb_count)),
-            dma((orb_count,)),
-            dma((orb_count,)),
-            dma((orb_count,)),
-            dma((orb_count,)),
-            dma(()),
+            dma((2, orb_count, parts)),
+            dma((2, orb_count, parts)),
+            dma((orb_count, parts)),
+            dma((orb_count, parts)),
+            dma((orb_count, parts)),
+            dma((orb_count, parts)),
+            dma((parts,)),
         ],
         compiler_params=pltpu.CompilerParams(
             collective_id=collective_id, has_side_effects=True, vmem_limit_bytes=VMEM_LIMIT
@@ -375,7 +393,9 @@
     )(contributions)
 
 
-def amplitude_kernel(first_ref, second_ref, shift_ref, left, right, col, row, out, total):
+def amplitude_kernel(
+    first_ref, second_ref, shift_ref, left, right, col, row, upper, lower, total
+):
     pair = pl.program_id(0)
     step = pl.program_id(1)
 
@@ -383,11 +403,12 @@
     def _():
         total[...] = jnp.zeros_like(total)
 
-    total[...] += dot3(left[0, 0], right[0, 0], ((0,), (0,)))
+    total[...] += dot3(split(left[0, 0]), split(right[0, 0]), ((0,), (0,)))
 
     @pl.when(step == pl.num_programs(1) - 1)
     def _():
-        out[0] = -total[...] / (col[...] + row[...] - shift_ref[pair])
+        amps = -total[...] / (col[...] + row[...] - shift_ref[pair])
+        upper[0], lower[0] = split(amps)
 
 
 def amplitudes_of(first_slot, second_slot, shift, slots, vir_energy):
@@ -404,16 +425,16 @@
                 pl.BlockSpec((cols, 1), lambda p, a, f, s, e: (0, 0)),
                 pl.BlockSpec((1, cols), lambda p, a, f, s, e: (0, 0)),
             ],
-            out_specs=pl.BlockSpec((1, cols, cols), lambda p, a, f, s, e: (p, 0, 0)),
+            out_specs=[pl.BlockSpec((1, cols, cols), lambda p, a, f, s, e: (p, 0, 0))] * 2,
             scratch_shapes=[pltpu.VMEM((cols, cols), f32)],
         ),
-        out_shape=jax.ShapeDtypeStruct((pairs, cols, cols), f32),
+        out_shape=[jax.ShapeDtypeStruct((pairs, cols, cols), bf16)] * 2,
         compiler_params=pltpu.CompilerParams(vmem_limit_bytes=VMEM_LIMIT),
         name="pair_amplitudes",
     )(first_slot, second_slot, shift, slots, slots, vir_energy[:, None], vir_energy[None, :])
 
 
-def contribution_kernel(first_ref, second_ref, slots, amps, out):
+def contribution_kernel(first_ref, second_ref, slots, upper, lower, out):
     slot = pl.program_id(1)
     out[0, 0] = jnp.zeros_like(out[0, 0])
 
@@ -423,15 +444,19 @@
 
         @pl.when(first == slot)
         def _():
-            out[0, 0] += dot3(slots[0, second], amps[pair], ((1,), (1,)))
+            out[0, 0] += dot3(
+                split(slots[0, second]), (upper[pair], lower[pair]), ((1,), (1,))
+            )
 
         @pl.when(second == slot)
         def _():
-            out[0, 0] += dot3(slots[0, first], amps[pair], ((1,), (0,)))
+            out[0, 0] += dot3(
+                split(slots[0, first]), (upper[pair], lower[pair]), ((1,), (0,))
+            )
 
         return carry
 
-    lax.fori_loop(0, amps.shape[0], visit, 0)
+    lax.fori_loop(0, upper.shape[0], visit, 0)
 
 
 def contributions_of(first_slot, second_slot, slots, amps):
@@ -443,14 +468,15 @@
             grid=(aux_count, orb_count),
             in_specs=[
                 pl.BlockSpec((1, orb_count, rows, cols), lambda a, o, f, s: (a, 0, 0, 0)),
-                pl.BlockSpec(amps.shape, lambda a, o, f, s: (0, 0, 0)),
+                pl.BlockSpec(amps[0].shape, lambda a, o, f, s: (0, 0, 0)),
+                pl.BlockSpec(amps[1].shape, lambda a, o, f, s: (0, 0, 0)),
             ],
             out_specs=pl.BlockSpec((1, 1, rows, cols), lambda a, o, f, s: (a, o, 0, 0)),
         ),
         out_shape=jax.ShapeDtypeStruct(slots.shape, f32),
         compiler_params=pltpu.CompilerParams(vmem_limit_bytes=VMEM_LIMIT),
         name="slot_contributions",
-    )(first_slot, second_slot, slots, amps)
+    )(first_slot, second_slot, slots, *amps)
 
 
 def body(integrals, metric, occ_energy, vir_energy, pair_orbitals):
@@ -459,10 +485,11 @@
     orb_count = lax.axis_size("orb")
     aux_index = lax.axis_index("aux")
     orb_index = lax.axis_index("orb")
-    pieces = 4
+    pieces = 8
+    halves = (2, aux_rows // 2, vir_count)
     columns = occ_count * vir_count
     all_rows = gather(
-        integrals.reshape(pieces, aux_rows // pieces, columns), aux_count, False, 1
+        integrals.reshape(pieces, 1, aux_rows // pieces, columns), aux_count, False, 1
     ).reshape(aux_count * aux_rows, columns)
     fitted = lax.dot_general(
         metric, all_rows, (((1,), (0,)), ((), ())), precision=high, preferred_element_type=f32
@@ -475,7 +502,8 @@
     for o in range(occ_count):
         part = fitted[:, o * vir_count : (o + 1) * vir_count]
         outgoing = jnp.where((wanted == o)[:, None, None], part[None], outgoing)
-    slots = gather(outgoing, aux_count, True, 2)
+    slots = gather(outgoing.reshape((orb_count,) + halves), aux_count, True, 2)
+    slots = slots.reshape(aux_count, orb_count, aux_rows, vir_count)
     my_count = pair_count // aux_count
     my_pairs = lax.dynamic_slice_in_dim(
         pair_orbitals, orb_index * pair_count + aux_index * my_count, my_count, 0
@@ -487,7 +515,8 @@
     shift = occ_energy[first_orb] + occ_energy[second_orb]
     amps = amplitudes_of(first_slot, second_slot, shift, slots, vir_energy)
     contributions = contributions_of(first_slot, second_slot, slots, amps)
-    received = give_back(contributions, 3)
+    received = give_back(contributions.reshape((aux_count, orb_count) + halves), 3)
+    received = received.reshape(orb_count, aux_rows, vir_count)
     outs = [
         jnp.sum(jnp.where((wanted == o)[:, None, None], received, 0.0), axis=0)
         for o in range(occ_count)

time: 624 us -> 578 us (0.926)
  Pallas kernels: 588 us -> 544 us
    pallas_call x2, Pallas kernels: 289 us -> 254 us  [gather(): pl.pallas_call(functools.partial(gather_kernel, count, y_count, exchange)...]
    pallas_call x1, Pallas kernels: 214 us -> 200 us  [give_back(): pl.pallas_call(functools.partial(return_kernel, orb_count), out_shape=jax...]
where the time goes in v2:
time: 578 us; the launch traced here: 577 us
  Pallas kernels  544 us (94%)
  other arithmetic  11.4 us (2%)
  local copies, waits for them, and re-layouts  10.8 us (2%)
  matrix products  10.8 us (2%)
    pallas_call x2, Pallas kernels, gather(): pl.pallas_call(functools.partial(gather_kernel, count, y_count, exchange)...  254 us
    pallas_call x1, Pallas kernels, give_back(): pl.pallas_call(functools.partial(return_kernel, orb_count), out_shape=jax...  200 us
    pallas_call x1, Pallas kernels, contributions_of(): pl.pallas_call(contribution_kernel, grid_spec=pltpu.PrefetchScalarGridSpe...  62.7 us
    pallas_call x1, Pallas kernels, amplitudes_of(): pl.pallas_call(amplitude_kernel, grid_spec=pltpu.PrefetchScalarGridSpec(n...  26.8 us

profile of v2, /device:TPU:0, one launch (start us, length us, event | category | flops | bytes accessed | tf_op | source)
XLA Modules:
  0.0 577.2 jit_solution(2285193368395052964)
XLA Ops:
  0.0 0.0 copy-start
  0.0 0.7 fusion
  0.7 0.8 constant_dynamic-slice_fusion
  1.5 0.6 and_select_fusion
  2.1 0.1 reduce_max.14
  2.1 0.1 reduce_max.18
  2.3 0.0 copy-done
  2.3 0.6 gather_fusion.1
  2.9 0.6 gather_fusion
  3.6 0.5 add.33.shift_ref
  4.1 1.5 copy.6.col
  5.7 4.0 reshape.32.x_ref
  9.7 51.8 %gather_aux.1 = f32[4,8,1,64,1024]{4,3,2,1,0:T(8,128)} custom-call(f32[8,1,64,1024]{3,2,1,0:T(8,128)} %reshape.32.x_ref), custom_call_target="tpu_custom_call" | custom-call | tf_op jit(solution)/shard_map/gather_aux/pallas_call | solution.py:212
  61.5 10.8 %fusion.4 = f32[512,1024]{1,0:T(8,128)S(1)} fusion(f32[512,2048]{1,0:T(8,128)} %param.6, f32[2048,1024]{1,0:T(8,128)} %bitcast.35), kind=kOutput, calls=%fused_computation.33 | convolution fusion | flops 6442450944 | bytes 14680064 | tf_op jit(solution)/shard_map/dot_general | solution.py:494
  72.4 0.2 fusion.3
  72.6 4.3 select_select_fusion.x_ref
  76.9 202.3 %gather_exchange.1 = f32[4,8,2,256,512]{4,3,2,1,0:T(8,128)} custom-call(f32[8,2,256,512]{3,2,1,0:T(8,128)} %select_select_fusion.x_ref), custom_call_target="tpu_custom_call" | custom-call | tf_op jit(solution)/shard_map/gather_exchange/pallas_call | solution.py:212
  279.2 26.8 %pair_amplitudes.1 = (bf16[4,512,512]{2,1,0:T(8,128)(2,1)}, bf16[4,512,512]{2,1,0:T(8,128)(2,1)}) custom-call(s32[4]{0:T(128)} %get-tuple-element.16.first_ref, s32[4]{0:T(128)} %get-tuple-element.15.second_ref, f32[4]{0:T(128)} %add.33.shift_ref, f32[4,8,512,512]{3,2,1,0:T(8,128)} %bitcast.31, f32[4,8,512,512]{3,2,1,0:T(8,128)} %bitcast.32, ...), custom_call_target="tpu_custom_call" | custom-call | tf_op jit(solution)/shard_map/pair_amplitudes/pallas_call | solution.py:417
  306.0 62.7 %slot_contributions.1 = f32[4,8,512,512]{3,2,1,0:T(8,128)} custom-call(s32[4]{0:T(128)} %get-tuple-element.16.first_ref, s32[4]{0:T(128)} %get-tuple-element.15.second_ref, f32[4,8,512,512]{3,2,1,0:T(8,128)} %bitcast.33, bf16[4,512,512]{2,1,0:T(8,128)(2,1)} %get-tuple-element.7.upper, bf16[4,512,512]{2,1,0:T(8,128)(2,1)} %get-tuple-element.8.lower), custom_call_target="tpu_custom_call" | custom-call | tf_op jit(solution)/shard_map/slot_contributions/pallas_call | solution.py:464
  368.7 200.4 %give_back.1 = f32[8,2,256,512]{3,2,1,0:T(8,128)} custom-call(f32[4,8,2,256,512]{4,3,2,1,0:T(8,128)} %bitcast.34), custom_call_target="tpu_custom_call" | custom-call | tf_op jit(solution)/shard_map/give_back/pallas_call | solution.py:370
  569.1 4.9 select_reduce_fusion.1
  574.0 0.0 copy-start.1
  574.0 0.2 pad_maximum_fusion
  574.2 2.9 copy.7
  577.1 0.0 copy-done.1
  (3 shorter events, 0.0 us)
Async XLA Ops:
  0.0 2.3 copy-start
  574.0 3.1 copy-start.1

commit v3 on v2

--- a/solution.py
+++ b/solution.py
@@ -229,6 +229,234 @@
         ),
         name="gather_exchange" if exchange else "gather_aux",
     )(blocks)
+
+
+def gateway_kernel(
+    hit_ref,
+    fit_ref,
+    x_ref,
+    out_ref,
+    both,
+    picks,
+    stage,
+    keep_sem,
+    f_send,
+    f_recv,
+    orb_send,
+    orb_recv,
+    y_send,
+    y_recv,
+    c_send,
+    c_recv,
+):
+    aux = lax.axis_index("aux")
+    orb = lax.axis_index("orb")
+    y = aux // 2
+    core = aux % 2
+    partner = 2 * y + 1 - core
+    across = 2 * (1 - y) + core
+    occ_count, parts, rows, _ = fit_ref.shape
+    gate = 6
+    tile = 64
+    passed = {1: 7, 2: 4, 3: 5}
+
+    def place_of(k):
+        return flip(orb, k, 8)
+
+    barrier = pltpu.get_barrier_semaphore()
+    for k in (1, 2, 3, gate):
+        pl.semaphore_signal(
+            barrier, inc=1, device_id={"aux": aux, "orb": place_of(k)}, device_id_type=MESH
+        )
+    for peer in (partner, across):
+        pl.semaphore_signal(
+            barrier, inc=1, device_id={"aux": peer, "orb": orb}, device_id_type=MESH
+        )
+    pl.semaphore_wait(barrier, 6)
+
+    def far_copy(o, h):
+        return pltpu.make_async_remote_copy(
+            src_ref=fit_ref.at[o, h],
+            dst_ref=both.at[o, h],
+            send_sem=f_send.at[o, h],
+            recv_sem=f_recv.at[o, h],
+            device_id={"aux": aux, "orb": place_of(gate)},
+            device_id_type=MESH,
+        )
+
+    def near_copy(k, h):
+        return pltpu.make_async_remote_copy(
+            src_ref=x_ref.at[k, h],
+            dst_ref=out_ref.at[aux, orb, h],
+            send_sem=orb_send.at[k, h],
+            recv_sem=orb_recv.at[k, h],
+            device_id={"aux": aux, "orb": place_of(k)},
+            device_id_type=MESH,
+        )
+
+    def pass_copy(d, h):
+        return pltpu.make_async_remote_copy(
+            src_ref=picks.at[d, h],
+            dst_ref=out_ref.at[aux, place_of(gate), h],
+            send_sem=orb_send.at[passed[d], h],
+            recv_sem=orb_recv.at[passed[d], h],
+            device_id={"aux": aux, "orb": place_of(d)},
+            device_id_type=MESH,
+        )
+
+    def own(k, h):
+        if k == 0:
+            return x_ref.at[0, h]
+        if k == gate:
+            return picks.at[0, h]
+        return out_ref.at[aux, place_of(k), h]
+
+    def y_copy(k, h):
+        return pltpu.make_async_remote_copy(
+            src_ref=own(k, h),
+            dst_ref=out_ref.at[aux, place_of(k), h],
+            send_sem=y_send.at[k, h],
+            recv_sem=y_recv.at[k, h],
+            device_id={"aux": across, "orb": orb},
+            device_id_type=MESH,
+        )
+
+    def core_copy(k, h):
+        return pltpu.make_async_remote_copy(
+            src_ref=own(k, h),
+            dst_ref=out_ref.at[aux, place_of(k), h],
+            send_sem=c_send.at[0, k, h],
+            recv_sem=c_recv.at[0, k, h],
+            device_id={"aux": partner, "orb": orb},
+            device_id_type=MESH,
+        )
+
+    def relay_copy(k, h):
+        return pltpu.make_async_remote_copy(
+            src_ref=out_ref.at[across, place_of(k), h],
+            dst_ref=out_ref.at[across, place_of(k), h],
+            send_sem=c_send.at[1, k, h],
+            recv_sem=c_recv.at[1, k, h],
+            device_id={"aux": partner, "orb": orb},
+            device_id_type=MESH,
+        )
+
+    def load(h):
+        return pltpu.make_async_copy(x_ref.at[0, h], stage.at[h], keep_sem.at[0, h])
+
+    def save(h):
+        return pltpu.make_async_copy(
+            stage.at[h], out_ref.at[aux, place_of(0), h], keep_sem.at[0, h]
+        )
+
+    def save_pick(h):
+        return pltpu.make_async_copy(
+            picks.at[0, h], out_ref.at[aux, place_of(gate), h], keep_sem.at[1, h]
+        )
+
+    def pick(h):
+        for o in range(occ_count):
+            far_copy(o, h).wait_recv()
+        for d in (2, 3, 1, 0):
+
+            def one(i, carry, d=d):
+                at = pl.ds(pl.multiple_of(i * tile, tile), tile)
+                total = both[0, h, at, :] * hit_ref[d, 0]
+                for o in range(1, occ_count):
+                    total = total + both[o, h, at, :] * hit_ref[d, o]
+                picks[d, h, at, :] = total
+                return carry
+
+            lax.fori_loop(0, rows // tile, one, 0)
+            if d:
+                pass_copy(d, h).start()
+            else:
+                save_pick(h).start()
+
+    for h in range(parts):
+        for o in range(occ_count):
+            far_copy(o, h).start()
+        for k in (1, 2, 3):
+            near_copy(k, h).start()
+        load(h).start()
+    units = [(k, h) for k in (0, 1, 2, 3, gate, 7, 4, 5) for h in range(parts)]
+    pending = []
+
+    def relay(k, h):
+        y_copy(k, h).wait_recv()
+        relay_copy(k, h).start()
+
+    for index, (k, h) in enumerate(units):
+        if k in (1, 2, 3):
+            near_copy(k, h).wait_recv()
+        elif k in (4, 5, 7):
+            pltpu.make_async_remote_copy(
+                src_ref=own(k, h),
+                dst_ref=own(k, h),
+                send_sem=orb_send.at[k, h],
+                recv_sem=orb_recv.at[k, h],
+                device_id={"aux": aux, "orb": place_of(gate)},
+                device_id_type=MESH,
+            ).wait_recv()
+        y_copy(k, h).start()
+        core_copy(k, h).start()
+        pending.append((k, h))
+        if len(pending) > 3:
+            relay(*pending.pop(0))
+        if index % parts == parts - 1 and index // parts < parts:
+            pick(index // parts)
+        if index == parts - 1:
+            for i in range(parts):
+                load(i).wait()
+                save(i).start()
+    for unit in pending:
+        relay(*unit)
+    for h in range(parts):
+        for o in range(occ_count):
+            far_copy(o, h).wait_send()
+        for k in (1, 2, 3):
+            near_copy(k, h).wait_send()
+            pass_copy(k, h).wait_send()
+        save(h).wait()
+        save_pick(h).wait()
+    for k, h in units:
+        core_copy(k, h).wait()
+        relay_copy(k, h).wait()
+        y_copy(k, h).wait_send()
+
+
+def gateway_exchange(hits, fitted, near, collective_id):
+    parts = near.shape[1]
+    piece = near.shape[2:]
+    dma = pltpu.SemaphoreType.DMA
+    return pl.pallas_call(
+        gateway_kernel,
+        out_shape=jax.ShapeDtypeStruct((4, 8, parts) + piece, f32),
+        in_specs=[
+            pl.BlockSpec(memory_space=pltpu.SMEM),
+            pl.BlockSpec(memory_space=pl.ANY),
+            pl.BlockSpec(memory_space=pl.ANY),
+        ],
+        out_specs=pl.BlockSpec(memory_space=pl.ANY),
+        scratch_shapes=[
+            pltpu.VMEM(fitted.shape, f32),
+            pltpu.VMEM((4, parts) + piece, f32),
+            pltpu.VMEM((parts,) + piece, f32),
+            dma((2, parts)),
+            dma(fitted.shape[:2]),
+            dma(fitted.shape[:2]),
+            dma((8, parts)),
+            dma((8, parts)),
+            dma((8, parts)),
+            dma((8, parts)),
+            dma((2, 8, parts)),
+            dma((2, 8, parts)),
+        ],
+        compiler_params=pltpu.CompilerParams(
+            collective_id=collective_id, has_side_effects=True, vmem_limit_bytes=VMEM_LIMIT
+        ),
+        name="gateway_exchange",
+    )(hits, fitted, near)
 
 
 def return_kernel(
@@ -486,7 +714,7 @@
     aux_index = lax.axis_index("aux")
     orb_index = lax.axis_index("orb")
     pieces = 8
-    halves = (2, aux_rows // 2, vir_count)
+    pieced = (4, aux_rows // 4, vir_count)
     columns = occ_count * vir_count
     all_rows = gather(
         integrals.reshape(pieces, 1, aux_rows // pieces, columns), aux_count, False, 1
@@ -498,11 +726,25 @@
     pair_ends = pair_orbitals.reshape(orb_count, 2 * pair_count)
     local_pick = jnp.where(pair_ends // occ_count == orb_index, pair_ends % occ_count, -1)
     wanted = jnp.max(local_pick, axis=1)
-    outgoing = jnp.zeros((orb_count, aux_rows, vir_count), f32)
-    for o in range(occ_count):
-        part = fitted[:, o * vir_count : (o + 1) * vir_count]
-        outgoing = jnp.where((wanted == o)[:, None, None], part[None], outgoing)
-    slots = gather(outgoing.reshape((orb_count,) + halves), aux_count, True, 2)
+    parted = [
+        fitted[:, o * vir_count : (o + 1) * vir_count].reshape(pieced) for o in range(occ_count)
+    ]
+
+    def choose(picked):
+        total = jnp.zeros(picked.shape + pieced, f32)
+        for o in range(occ_count):
+            total = jnp.where((picked == o)[:, None, None, None], parted[o][None], total)
+        return total
+
+    if orb_count == 8 and occ_count < 4:
+        half = jnp.stack([flip(orb_index, k, 8) for k in range(4)])
+        gate = flip(orb_index, 6, 8)
+        gate_pick = jnp.where(pair_ends // occ_count == gate, pair_ends % occ_count, -1)
+        gate_wanted = jnp.max(gate_pick, axis=1)[half]
+        hits = (gate_wanted[:, None] == jnp.arange(occ_count, dtype=jnp.int32)[None, :]).astype(f32)
+        slots = gateway_exchange(hits, jnp.stack(parted), choose(wanted[half]), 2)
+    else:
+        slots = gather(choose(wanted), aux_count, True, 2)
     slots = slots.reshape(aux_count, orb_count, aux_rows, vir_count)
     my_count = pair_count // aux_count
     my_pairs = lax.dynamic_slice_in_dim(
@@ -515,13 +757,12 @@
     shift = occ_energy[first_orb] + occ_energy[second_orb]
     amps = amplitudes_of(first_slot, second_slot, shift, slots, vir_energy)
     contributions = contributions_of(first_slot, second_slot, slots, amps)
-    received = give_back(contributions.reshape((aux_count, orb_count) + halves), 3)
+    received = give_back(contributions.reshape((aux_count, orb_count) + pieced), 3)
     received = received.reshape(orb_count, aux_rows, vir_count)
-    outs = [
-        jnp.sum(jnp.where((wanted == o)[:, None, None], received, 0.0), axis=0)
-        for o in range(occ_count)
-    ]
-    return jnp.stack(outs, axis=1)
+    keep = wanted[:, None] == jnp.arange(occ_count, dtype=jnp.int32)[None, :]
+    return jnp.sum(
+        jnp.where(keep[:, None, :, None], received[:, :, None, :], 0.0), axis=0
+    )
 
 
 def plain_body(integrals, metric, occ_energy, vir_energy, pair_orbitals):

time: 578 us -> 584 us (1.010)
  Pallas kernels: 544 us -> 550 us
    pallas_call x0 -> x1, Pallas kernels: none -> 213 us  [gateway_exchange(): pl.pallas_call(gateway_kernel, out_shape=jax.ShapeDtypeStruct((4, 8, part...]
    pallas_call x2 -> x1, Pallas kernels: 254 us -> 51.8 us  [gather(): pl.pallas_call(functools.partial(gather_kernel, count, y_count, exchange)...]
where the time goes in v3:
time: 584 us; the launch traced here: 583 us
  Pallas kernels  550 us (94%)
  other arithmetic  11.9 us (2%)
  local copies, waits for them, and re-layouts  10.8 us (2%)
  matrix products  10.8 us (2%)
    pallas_call x1, Pallas kernels, gateway_exchange(): pl.pallas_call(gateway_kernel, out_shape=jax.ShapeDtypeStruct((4, 8, part...  213 us
    pallas_call x1, Pallas kernels, give_back(): pl.pallas_call(functools.partial(return_kernel, orb_count), out_shape=jax...  200 us
    pallas_call x1, Pallas kernels, contributions_of(): pl.pallas_call(contribution_kernel, grid_spec=pltpu.PrefetchScalarGridSpe...  58.6 us
    pallas_call x1, Pallas kernels, gather(): pl.pallas_call(functools.partial(gather_kernel, count, y_count, exchange)...  51.8 us
    pallas_call x1, Pallas kernels, amplitudes_of(): pl.pallas_call(amplitude_kernel, grid_spec=pltpu.PrefetchScalarGridSpec(n...  26.2 us

profile of v3, /device:TPU:0, one launch (start us, length us, event | category | flops | bytes accessed | tf_op | source)
XLA Modules:
  0.0 583.3 jit_solution(538222709777792954)
XLA Ops:
  0.0 0.0 copy-start
  0.0 0.1 fusion.3
  0.1 0.7 fusion.1
  0.8 0.1 reduce_max.24
  0.9 0.1 reduce_max.25
  1.0 0.6 gather_fusion.1
  1.7 4.0 reshape.206.x_ref
  5.7 51.8 %gather_aux.1 = f32[4,8,1,64,1024]{4,3,2,1,0:T(8,128)} custom-call(f32[8,1,64,1024]{3,2,1,0:T(8,128)} %reshape.206.x_ref), custom_call_target="tpu_custom_call" | custom-call | tf_op jit(solution)/shard_map/gather_aux/pallas_call | solution.py:212
  57.5 10.8 %fusion.7 = f32[512,1024]{1,0:T(8,128)S(1)} fusion(f32[512,2048]{1,0:T(8,128)} %param.6, f32[2048,1024]{1,0:T(8,128)} %bitcast.47), kind=kOutput, calls=%fused_computation.44 | convolution fusion | flops 6442450944 | bytes 14680064 | tf_op jit(solution)/shard_map/dot_general | solution.py:722
  68.4 0.2 fusion.6
  68.6 2.7 select_select_fusion.x_ref
  71.2 0.1 reduce_max.36
  71.3 0.1 reduce_max.37
  71.4 0.6 gather_fusion
  72.1 0.6 fusion.hit_ref
  72.7 1.5 pad_maximum_fusion.fit_ref
  74.2 213.4 %gateway_exchange.1 = f32[4,8,4,128,512]{4,3,2,1,0:T(8,128)} custom-call(f32[4,2]{1,0:T(4,128)} %fusion.hit_ref, f32[2,4,128,512]{3,2,1,0:T(8,128)} %pad_maximum_fusion.fit_ref, f32[4,4,128,512]{3,2,1,0:T(8,128)} %select_select_fusion.x_ref), custom_call_target="tpu_custom_call" | custom-call | tf_op jit(solution)/shard_map/gateway_exchange/pallas_call | solution.py:432
  287.6 0.0 copy-done.3
  287.6 0.1 constant_dynamic-slice_fusion
  287.7 0.0 copy-done
  287.7 0.6 gather_fusion.2
  288.3 0.6 gather_fusion.3
  289.0 0.6 add.138.shift_ref
  289.6 0.6 and_select_fusion
  290.1 0.9 copy.7.col
  291.0 26.2 %pair_amplitudes.1 = (bf16[4,512,512]{2,1,0:T(8,128)(2,1)}, bf16[4,512,512]{2,1,0:T(8,128)(2,1)}) custom-call(s32[4]{0:T(128)} %get-tuple-element.16.first_ref, s32[4]{0:T(128)} %get-tuple-element.15.second_ref, f32[4]{0:T(128)} %add.138.shift_ref, f32[4,8,512,512]{3,2,1,0:T(8,128)} %bitcast.38, f32[4,8,512,512]{3,2,1,0:T(8,128)} %bitcast.39, ...), custom_call_target="tpu_custom_call" | custom-call | tf_op jit(solution)/shard_map/pair_amplitudes/pallas_call | solution.py:645
  317.2 58.6 %slot_contributions.1 = f32[4,8,512,512]{3,2,1,0:T(8,128)} custom-call(s32[4]{0:T(128)} %get-tuple-element.16.first_ref, s32[4]{0:T(128)} %get-tuple-element.15.second_ref, f32[4,8,512,512]{3,2,1,0:T(8,128)} %bitcast.40, bf16[4,512,512]{2,1,0:T(8,128)(2,1)} %get-tuple-element.7.upper, bf16[4,512,512]{2,1,0:T(8,128)(2,1)} %get-tuple-element.8.lower), custom_call_target="tpu_custom_call" | custom-call | tf_op jit(solution)/shard_map/slot_contributions/pallas_call | solution.py:692
  375.8 199.6 %give_back.1 = f32[8,4,128,512]{3,2,1,0:T(8,128)} custom-call(f32[4,8,4,128,512]{4,3,2,1,0:T(8,128)} %bitcast.41), custom_call_target="tpu_custom_call" | custom-call | tf_op jit(solution)/shard_map/give_back/pallas_call | solution.py:598
  575.4 0.1 iota_compare_fusion
  575.5 4.8 select_reduce_fusion
  580.3 2.9 copy.8
  583.3 0.0 copy-done.1
  (8 shorter events, 0.0 us)
Async XLA Ops:
  0.0 287.7 %copy-start = (f32[16]{0:T(128)S(1)}, f32[16]{0:T(128)}, u32[]{:S(2)}) copy-start(f32[16]{0:T(128)} %param.7) | copy-start | bytes 196
  74.2 213.4 %copy-start.3 = (s32[128,2]{0,1:T(2,128)S(1)}, s32[128,2]{0,1:T(2,128)}, u32[]{:S(2)}) copy-start(s32[128,2]{0,1:T(2,128)} %param.9) | copy-start | bytes 3076
  74.2 216.0 %copy-start.2 = (f32[512]{0:T(512)S(1)}, f32[512]{0:T(512)}, u32[]{:S(2)}) copy-start(f32[512]{0:T(512)} %param.8) | copy-start | bytes 6148
  575.5 7.8 %copy-start.1 = (f32[16]{0:T(128)S(1)}, f32[16]{0:T(128)}, u32[]{:S(2)}) copy-start(f32[16]{0:T(128)} %param.7) | copy-start | bytes 196

commit v4 on v2

--- a/solution.py
+++ b/solution.py
@@ -486,7 +486,7 @@
     aux_index = lax.axis_index("aux")
     orb_index = lax.axis_index("orb")
     pieces = 8
-    halves = (2, aux_rows // 2, vir_count)
+    halves = (4, aux_rows // 4, vir_count)
     columns = occ_count * vir_count
     all_rows = gather(
         integrals.reshape(pieces, 1, aux_rows // pieces, columns), aux_count, False, 1

time: 578 us -> 569 us (0.984)
  Pallas kernels: 544 us -> 536 us
where the time goes in v4:
time: 569 us
  Pallas kernels  536 us (94%)
  other arithmetic  11.4 us (2%)
  local copies, waits for them, and re-layouts  10.8 us (2%)
  matrix products  10.8 us (2%)
    pallas_call x2, Pallas kernels, gather(): pl.pallas_call(functools.partial(gather_kernel, count, y_count, exchange)...  249 us
    pallas_call x1, Pallas kernels, give_back(): pl.pallas_call(functools.partial(return_kernel, orb_count), out_shape=jax...  200 us
    pallas_call x1, Pallas kernels, contributions_of(): pl.pallas_call(contribution_kernel, grid_spec=pltpu.PrefetchScalarGridSpe...  60.5 us
    pallas_call x1, Pallas kernels, amplitudes_of(): pl.pallas_call(amplitude_kernel, grid_spec=pltpu.PrefetchScalarGridSpec(n...  26.2 us

profile of v4, /device:TPU:0, one launch (start us, length us, event | category | flops | bytes accessed | tf_op | source)
XLA Modules:
  0.0 568.8 jit_solution(17113374933477638337)
XLA Ops:
  0.0 0.0 copy-start
  0.0 0.7 fusion
  0.7 0.8 constant_dynamic-slice_fusion
  1.5 0.6 and_select_fusion
  2.1 0.1 reduce_max.14
  2.1 0.1 reduce_max.18
  2.3 0.0 copy-done
  2.3 0.6 gather_fusion.1
  2.9 0.6 gather_fusion
  3.6 0.5 add.33.shift_ref
  4.1 1.5 copy.6.col
  5.7 4.0 reshape.32.x_ref
  9.7 51.8 %gather_aux.1 = f32[4,8,1,64,1024]{4,3,2,1,0:T(8,128)} custom-call(f32[8,1,64,1024]{3,2,1,0:T(8,128)} %reshape.32.x_ref), custom_call_target="tpu_custom_call" | custom-call | tf_op jit(solution)/shard_map/gather_aux/pallas_call | solution.py:212
  61.5 10.8 %fusion.4 = f32[512,1024]{1,0:T(8,128)S(1)} fusion(f32[512,2048]{1,0:T(8,128)} %param.6, f32[2048,1024]{1,0:T(8,128)} %bitcast.35), kind=kOutput, calls=%fused_computation.33 | convolution fusion | flops 6442450944 | bytes 14680064 | tf_op jit(solution)/shard_map/dot_general | solution.py:494
  72.4 0.2 fusion.3
  72.6 4.3 select_select_fusion.x_ref
  76.9 197.5 %gather_exchange.1 = f32[4,8,4,128,512]{4,3,2,1,0:T(8,128)} custom-call(f32[8,4,128,512]{3,2,1,0:T(8,128)} %select_select_fusion.x_ref), custom_call_target="tpu_custom_call" | custom-call | tf_op jit(solution)/shard_map/gather_exchange/pallas_call | solution.py:212
  274.4 26.2 %pair_amplitudes.1 = (bf16[4,512,512]{2,1,0:T(8,128)(2,1)}, bf16[4,512,512]{2,1,0:T(8,128)(2,1)}) custom-call(s32[4]{0:T(128)} %get-tuple-element.16.first_ref, s32[4]{0:T(128)} %get-tuple-element.15.second_ref, f32[4]{0:T(128)} %add.33.shift_ref, f32[4,8,512,512]{3,2,1,0:T(8,128)} %bitcast.31, f32[4,8,512,512]{3,2,1,0:T(8,128)} %bitcast.32, ...), custom_call_target="tpu_custom_call" | custom-call | tf_op jit(solution)/shard_map/pair_amplitudes/pallas_call | solution.py:417
  300.6 60.5 %slot_contributions.1 = f32[4,8,512,512]{3,2,1,0:T(8,128)} custom-call(s32[4]{0:T(128)} %get-tuple-element.16.first_ref, s32[4]{0:T(128)} %get-tuple-element.15.second_ref, f32[4,8,512,512]{3,2,1,0:T(8,128)} %bitcast.33, bf16[4,512,512]{2,1,0:T(8,128)(2,1)} %get-tuple-element.7.upper, bf16[4,512,512]{2,1,0:T(8,128)(2,1)} %get-tuple-element.8.lower), custom_call_target="tpu_custom_call" | custom-call | tf_op jit(solution)/shard_map/slot_contributions/pallas_call | solution.py:464
  361.1 199.6 %give_back.1 = f32[8,4,128,512]{3,2,1,0:T(8,128)} custom-call(f32[4,8,4,128,512]{4,3,2,1,0:T(8,128)} %bitcast.34), custom_call_target="tpu_custom_call" | custom-call | tf_op jit(solution)/shard_map/give_back/pallas_call | solution.py:370
  560.7 4.9 select_reduce_fusion.1
  565.7 0.0 copy-start.1
  565.7 0.2 pad_maximum_fusion
  565.9 2.9 copy.7
  568.8 0.0 copy-done.1
  (3 shorter events, 0.0 us)
Async XLA Ops:
  0.0 2.3 copy-start
  565.7 3.1 copy-start.1
